TPU v7x, 32 devices: a whole 2x2x4 slice. The times are simulated.
32 devices in a mesh: seq: 4 (over x, core), mp: 8 (over z, y).
Axes of the slice: x: 2, y: 2, z: 4, core: 2. Of those that a mesh axis runs over, the one named last changes fastest.
Arguments:
- queries: bfloat16 [1024, 4096], P('seq', 'mp'), may hold values from -15 to 15
- keys_values: bfloat16 [2, 1024, 4096], P(None, 'seq', 'mp'), may hold values from -6 to 6
- residual: bfloat16 [1024, 4096], P('seq', 'mp'), may hold values from -6 to 6
- cotangent: bfloat16 [1024, 4096], P('seq', 'mp'), may hold values from -6 to 6
- out_weight: bfloat16 [2, 4096, 4096], P(None, 'mp'), may hold values from -0.09375 to 0.09375
- kv_weight: bfloat16 [2, 4096, 4096], P(None, None, 'mp'), may hold values from -0.09375 to 0.09375
- bounds: int32 [2, 1024], replicated, may hold values from 0 to 767, as said below
- windows: int32 [64], P('mp'), may hold values from 1 to 127, as said below
Outputs:
- states_out: bfloat16 [1024, 4096], P('seq', 'mp')
- grad_states: bfloat16 [1024, 4096], P('seq', 'mp')
Inputs may be any that keep to these rules, and one draw needn't show every extreme that they name: The encoder rows form 4 documents, each a run of consecutive positions; an encoder token's bounds are its own document's first and last position. The last document begins among the last 255 encoder positions. Decoder tokens belong to documents in reverse order, the first decoder token to the last document (other documents may have none), and carry that document's encoder bounds. `windows`: some head reaches exactly 127.
All inputs are finite; a program needn't handle non-finite values.
Results may differ from a plain program's by a relative error of at most 0.038.
Values may be sent and summed in bfloat16 or wider, within the bound.
A program may use at most 64 MiB of HBM per device.

v0:
```python
import jax
import jax.numpy as jnp
from jax import lax
from jax.sharding import PartitionSpec as P

HD = 64
WIN = 127


def with_halo(cells, sides, width):
    for axis, dim in sides:
        count = lax.axis_size(axis)
        ends = count - 1
        head = lax.slice_in_dim(cells, 0, width, axis=dim)
        tail = lax.slice_in_dim(cells, cells.shape[dim] - width, cells.shape[dim], axis=dim)
        cells = jnp.concatenate(
            [
                lax.ppermute(tail, axis, [(i, (i + 1) % count) for i in range(ends)]),
                cells,
                lax.ppermute(head, axis, [((i + 1) % count, i) for i in range(ends)]),
            ],
            axis=dim,
        )
    return cells


def softmax_masked(scores, permitted):
    masked_scores = jnp.where(permitted, scores, -jnp.inf)
    row_top = jnp.max(masked_scores, axis=-1, keepdims=True)
    exp_scores = jnp.exp(masked_scores - row_top)
    return exp_scores / jnp.sum(exp_scores, axis=-1, keepdims=True)


def shards(queries, keys_values, residual, cotangent, out_weight, kv_weight, bounds, windows):
    row_count = queries.shape[0]
    col_count = queries.shape[1]
    head_count = col_count // HD
    slab_count = lax.axis_size("seq")
    enc_slabs = 3 * slab_count // 4
    dec_slabs = slab_count - enc_slabs
    enc_tokens = enc_slabs * row_count
    token_count = slab_count * row_count
    dec_tokens = token_count - enc_tokens
    slab_index = lax.axis_index("seq")
    is_enc = slab_index < enc_slabs
    score_scale = HD ** (-0.5)
    own_pos = slab_index * row_count + jnp.arange(row_count, dtype=jnp.int32)
    own_first = lax.dynamic_slice_in_dim(bounds[0], slab_index * row_count, row_count)
    own_last = lax.dynamic_slice_in_dim(bounds[1], slab_index * row_count, row_count)
    query_heads = queries.reshape(row_count, head_count, HD)
    slice_cols = residual.shape[1]
    res_full, cot_full = (
        lax.all_gather(residual, "mp", axis=1, tiled=True),
        lax.all_gather(cotangent, "mp", axis=1, tiled=True),
    )
    model_width = cot_full.shape[1]
    rim_keys = with_halo(keys_values, (("seq", 1),), WIN)

    def local_part():
        span_count = rim_keys.shape[1]
        key_pos = slab_index * row_count - WIN + jnp.arange(span_count, dtype=jnp.int32)
        key_heads = rim_keys[0].reshape(span_count, head_count, HD)
        value_heads = rim_keys[1].reshape(span_count, head_count, HD)
        scores = (
            jnp.einsum("qhd,khd->hqk", query_heads, key_heads, preferred_element_type=jnp.float32)
            * score_scale
        )
        in_document = (key_pos[None, :] >= own_first[:, None]) & (
            key_pos[None, :] <= own_last[:, None]
        )
        distance = jnp.abs(own_pos[:, None] - key_pos[None, :])
        permitted = in_document[None] & (distance[None] <= windows[:, None, None])
        rounded = softmax_masked(scores, permitted).astype(jnp.bfloat16)
        context = jnp.einsum(
            "hqk,khd->qhd", rounded, value_heads, preferred_element_type=jnp.float32
        ).astype(jnp.bfloat16)
        return jnp.dot(
            context.reshape(row_count, col_count), out_weight[0], preferred_element_type=jnp.float32
        )

    head_partial = lax.cond(
        is_enc, local_part, lambda: jnp.zeros((row_count, model_width), jnp.float32)
    )
    attn_sum = lax.psum(head_partial.astype(jnp.bfloat16), "mp").astype(jnp.float32)
    hidden_full = (res_full.astype(jnp.float32) + attn_sum).astype(jnp.bfloat16)
    encoder_out = lax.dynamic_slice_in_dim(
        hidden_full, lax.axis_index("mp") * slice_cols, slice_cols, 1
    )

    def project_keys():
        key_proj = jnp.dot(hidden_full, kv_weight[0], preferred_element_type=jnp.float32).astype(
            jnp.bfloat16
        )
        value_proj = jnp.dot(hidden_full, kv_weight[1], preferred_element_type=jnp.float32).astype(
            jnp.bfloat16
        )
        return jnp.stack([key_proj, value_proj])

    cross_kv = lax.cond(
        is_enc, project_keys, lambda: jnp.zeros((2, row_count, col_count), jnp.bfloat16)
    )

    def context_gradient():
        return lax.dot_general(
            cot_full, out_weight[1], (((1,), (1,)), ((), ())), preferred_element_type=jnp.float32
        ).astype(jnp.bfloat16)

    dec_queries = lax.all_gather(queries, "seq", axis=0, tiled=True)[enc_tokens:]
    dec_heads = dec_queries.reshape(dec_tokens, head_count, HD)
    dec_first = bounds[0, enc_tokens:]
    dec_last = bounds[1, enc_tokens:]
    in_document = (own_pos[None, :] >= dec_first[:, None]) & (own_pos[None, :] <= dec_last[:, None])
    key_heads = cross_kv[0].reshape(row_count, head_count, HD)
    value_heads = cross_kv[1].reshape(row_count, head_count, HD)
    scores = (
        jnp.einsum("qhd,khd->hqk", dec_heads, key_heads, preferred_element_type=jnp.float32)
        * score_scale
    )
    masked_scores = jnp.where(in_document[None], scores, -jnp.inf)
    row_top = lax.pmax(jnp.max(masked_scores, axis=2), "seq")
    exp_scores = jnp.exp(masked_scores - row_top[:, :, None])
    row_total = lax.psum(jnp.sum(exp_scores, axis=2), "seq")
    weights = exp_scores / row_total[:, :, None]
    rounded = weights.astype(jnp.bfloat16)
    partial_ctx = jnp.einsum(
        "hqk,khd->qhd", rounded, value_heads, preferred_element_type=jnp.float32
    ).reshape(dec_tokens, col_count)
    context_all = lax.psum(partial_ctx.astype(jnp.bfloat16), "seq")
    dec_offset = jnp.maximum(slab_index - enc_slabs, 0) * row_count
    context = lax.dynamic_slice_in_dim(context_all, dec_offset, row_count, 0)
    out_part = lax.cond(
        is_enc,
        lambda: jnp.zeros((row_count, model_width), jnp.float32),
        lambda: jnp.dot(context, out_weight[1], preferred_element_type=jnp.float32),
    )
    grad_own = lax.cond(
        is_enc, lambda: jnp.zeros((row_count, col_count), jnp.bfloat16), context_gradient
    )
    grad_all = lax.all_gather(grad_own, "seq", axis=0, tiled=True)[enc_tokens:]
    grad_heads = grad_all.reshape(dec_tokens, head_count, HD)
    row_dots = jnp.einsum(
        "qhd,qhd->hq",
        grad_heads,
        context_all.reshape(dec_tokens, head_count, HD),
        preferred_element_type=jnp.float32,
    )
    prob_grad = jnp.einsum(
        "qhd,khd->hqk", grad_heads, value_heads, preferred_element_type=jnp.float32
    )
    score_grad = (weights * (prob_grad - row_dots[:, :, None])).astype(jnp.bfloat16)
    grad_blocks = score_grad.reshape(head_count, dec_slabs, row_count, row_count)
    prob_blocks = rounded.reshape(head_count, dec_slabs, row_count, row_count)
    query_blocks = dec_heads.reshape(dec_slabs, row_count, head_count, HD)
    grad_rows = grad_heads.reshape(dec_slabs, row_count, head_count, HD)
    key_parts = (
        score_scale
        * jnp.einsum(
            "hsqk,sqhd->skhd", grad_blocks, query_blocks, preferred_element_type=jnp.float32
        )
    ).astype(jnp.bfloat16)
    value_parts = jnp.einsum(
        "hsqk,sqhd->skhd", prob_blocks, grad_rows, preferred_element_type=jnp.float32
    ).astype(jnp.bfloat16)
    key_grad = (
        jnp.sum(key_parts.astype(jnp.float32), axis=0)
        .astype(jnp.bfloat16)
        .reshape(row_count, col_count)
    )
    value_grad = (
        jnp.sum(value_parts.astype(jnp.float32), axis=0)
        .astype(jnp.bfloat16)
        .reshape(row_count, col_count)
    )
    query_terms = score_scale * jnp.einsum(
        "hqk,khd->qhd", score_grad, key_heads, preferred_element_type=jnp.float32
    )
    query_sum = lax.psum(
        query_terms.reshape(dec_tokens, col_count).astype(jnp.bfloat16), "seq"
    ).astype(jnp.float32)
    query_grad = lax.dynamic_slice_in_dim(query_sum, dec_offset, row_count, 0).astype(jnp.bfloat16)
    contract = (((1,), (1,)), ((), ()))
    grad_terms = lax.dot_general(
        key_grad, kv_weight[0], contract, preferred_element_type=jnp.float32
    ) + lax.dot_general(value_grad, kv_weight[1], contract, preferred_element_type=jnp.float32)
    final_term = jnp.where(is_enc, grad_terms, out_part)
    final_share = lax.psum_scatter(
        final_term.astype(jnp.bfloat16), "mp", scatter_dimension=1, tiled=True
    ).astype(jnp.float32)
    base_rows = jnp.where(is_enc, cotangent, residual).astype(jnp.float32)
    final_rows = (base_rows + final_share).astype(jnp.bfloat16)
    states_out = jnp.where(is_enc, encoder_out, final_rows)
    grad_states = jnp.where(is_enc, final_rows, query_grad)
    return (states_out, grad_states)


def solution(mesh):
    return jax.shard_map(
        shards,
        mesh=mesh,
        in_specs=(
            P("seq", "mp"),
            P(None, "seq", "mp"),
            P("seq", "mp"),
            P("seq", "mp"),
            P(None, "mp", None),
            P(None, None, "mp"),
            P(),
            P("mp"),
        ),
        out_specs=(P("seq", "mp"), P("seq", "mp")),
        check_vma=False,
    )
```

profile of v0, /device:TPU:0, one launch (start us, length us, event | category | flops | bytes accessed | tf_op | source)
XLA Modules:
  0.0 340.2 jit_solution(7236549203202645054)
XLA Ops:
  8.0 0.0 all-gather.7.cloned.1.call-start
  8.1 0.7 all-gather.7.cloned.1.call-update
  8.8 0.0 all-reduce.4.cloned.1.call-start
  8.8 1.2 copy.30
  10.1 0.1 fusion.57
  10.2 2.4 collective-permute-start
  12.6 1.3 collective-permute-start.1
  13.9 4.2 %collective-permute-done.1 = bf16[2,127,512]{1,2,0:T(8,128)(2,1)S(1)} collective-permute-done((bf16[2,127,512]{1,2,0:T(8,128)(2,1)S(1)}, bf16[2,127,512]{1,2,0:T(8,128)(2,1)S(1)}, u32[]{:S(2)}, u32[]{:S(2)}) %collective-permute-start.1) | collective-permute-done | bytes 260128 | tf_op jit(solution)/shard_map/ppermute | solution.py:20
  18.1 0.5 pad_maximum_fusion
  18.7 8.5 %conditional.4 = (bf16[256,4096]{1,0:T(8,128)(2,1)S(1)}) conditional(s32[]{:T(128)} %convert_element_type.116, () %tuple.47, (s32[]{:T(128)}, s32[2,1024]{1,0:T(2,128)S(1)}, s32[]{:T(128)}, s32[256]{0:T(256)S(1)}, s32[8]{0:T(128)S(1)}, /*index=5*/bf16[256,512]{1,0:T(8,128)(2,1)S(1)}, bf16[2,510,512]{1,2,0:T(8,128)(2,1)S(1)}, ...), branch_computations={%region_0.0_spmd, %region_1.4_spmd} | conditional | flops 1489188096 | bytes 13526646 | solution.py:81
  18.8 0.1 constant_dynamic-slice_fusion
  18.9 0.2 compare_and_fusion
  19.0 0.1 copy.33
  19.2 0.1 subtract_abs_fusion
  19.3 0.1 fusion.54
  19.4 2.0 fusion.56
  21.5 2.3 fusion.11
  23.7 3.5 %fusion.1 = bf16[256,4096]{1,0:T(8,128)(2,1)S(1)} fusion(bf16[256,512]{0,1:T(8,128)(2,1)S(1)} %bitcast.107, bf16[2,512,4096]{2,1,0:T(8,128)(2,1)} %get-tuple-element.145), kind=kOutput, calls=%fused_computation.1 | convolution fusion | flops 1073741824 | bytes 6553600 | tf_op jit(solution)/shard_map/cond/branch_1_fun/dot_general | solution.py:77
  27.2 1.3 copy-done.2
  28.6 0.0 all-gather.5.cloned.1.call-start
  28.7 0.7 all-gather.5.cloned.1.call-update
  29.4 0.0 all-gather.9.cloned.1.call-start
  29.4 0.7 all-gather.9.cloned.1.call-update
  30.1 0.0 all-reduce.6.cloned.1.call-start
  30.2 0.1 compare_and_fusion.1
  30.3 0.0 all-gather.7.cloned.1.call-done
  30.3 1.0 slice.90
  31.3 0.1 copy.34
  31.4 136.0 %all-reduce.4.cloned.1.call-done = bf16[256,4096]{1,0:T(8,128)(2,1)} async-done(((bf16[256,4096]{1,0:T(8,128)(2,1)}), bf16[256,4096]{1,0:T(8,128)(2,1)}) %all-reduce.4.cloned.1.call-update) | async-done | bytes 2097168 | tf_op jit(solution)/shard_map/psum | solution.py:84
  167.4 4.3 %add_convert_fusion = bf16[256,4096]{1,0:T(8,128)(2,1)} fusion(bf16[256,4096]{1,0:T(8,128)(2,1)} %all-reduce.4.cloned.1.call-done, bf16[256,4096]{1,0:T(8,128)(2,1)} %all-gather.5.cloned.1.call-done), kind=kLoop, calls=%fused_computation.49 | loop fusion | flops 4194304 | bytes 6291456 | tf_op jit(solution)/shard_map/convert_element_type | solution.py:85
  171.8 8.3 %conditional.5 = (bf16[256,8,64]{0,2,1:T(8,128)(2,1)S(1)}, bf16[256,8,64]{0,2,1:T(8,128)(2,1)S(1)}) conditional(s32[]{:T(128)} %convert_element_type.116, () %tuple.49, (bf16[2,4096,512]{2,1,0:T(8,128)(2,1)}, bf16[256,4096]{1,0:T(8,128)(2,1)}) %tuple.50), branch_computations={%region_5.6_spmd, %region_6.7_spmd} | conditional | flops 2147745792 | bytes 47710252 | solution.py:99
  171.8 4.2 %fusion.29 = bf16[256,512]{1,0:T(8,128)(2,1)S(1)} fusion(bf16[256,4096]{1,0:T(8,128)(2,1)} %get-tuple-element.146, bf16[2,4096,512]{2,1,0:T(8,128)(2,1)} %get-tuple-element.147), kind=kOutput, calls=%fused_computation.33 | convolution fusion | flops 1073872896 | bytes 6553600 | tf_op jit(solution)/shard_map/cond/branch_1_fun/dot_general | solution.py:94
  176.0 1.0 copy-done.1
  177.0 2.8 fusion.26
  179.8 0.1 copy.28
  180.0 0.1 copy.29
  180.1 0.5 fusion.59
  180.7 5.8 %pmax.7 = f32[8,256]{1,0:T(8,128)S(1)} all-reduce(f32[8,256]{1,0:T(8,128)S(1)} %get-tuple-element.190), channel_id=1, replica_groups=mesh['seq'=4,'mp'=8] {'seq'}, use_global_device_ids=true, to_apply=%region_8.9 | all-reduce | flops 2048 | bytes 16384 | tf_op jit(solution)/shard_map/pmax | solution.py:120
  186.4 0.3 fusion.49
  186.7 6.7 %psum.29 = f32[8,256]{1,0:T(8,128)S(1)} all-reduce(f32[8,256]{1,0:T(8,128)S(1)} %fusion.49), channel_id=1, replica_groups=mesh['seq'=4,'mp'=8] {'seq'}, use_global_device_ids=true, to_apply=%region_10.11 | all-reduce | flops 2048 | bytes 16384 | tf_op jit(solution)/shard_map/psum | solution.py:122
  193.4 0.3 fusion.52
  193.7 1.0 convolution_convert_fusion.1
  194.8 0.0 all-gather.11.cloned.1.call-start
  194.9 0.2 conditional.6
  195.1 0.7 copy-done.12
  195.8 0.0 all-reduce.8.cloned.1.call-start
  195.9 29.9 %all-reduce.6.cloned.1.call-done = bf16[256,512]{0,1:T(8,128)(2,1)} async-done(((bf16[256,512]{0,1:T(8,128)(2,1)}), bf16[256,512]{0,1:T(8,128)(2,1)}) %all-reduce.6.cloned.1.call-update) | async-done | bytes 262160 | tf_op jit(solution)/shard_map/psum | solution.py:128
  225.8 1.5 conditional.7
  225.8 1.5 broadcast.157
  227.3 17.2 %all-gather.11.cloned.1.call-done = bf16[1024,512]{1,0:T(8,128)(2,1)} async-done(((bf16[256,512]{1,0:T(8,128)(2,1)}), bf16[1024,512]{1,0:T(8,128)(2,1)}) %all-gather.11.cloned.1.call-update) | async-done | bytes 1048592 | tf_op jit(solution)/shard_map/all_gather | solution.py:139
  244.5 1.7 slice.91
  246.2 1.1 copy.35
  247.3 1.1 convolution_convert_fusion
  248.4 1.0 fusion.53
  249.5 1.7 multiply_convert_fusion
  251.2 0.3 fusion.51
  251.5 0.4 fusion.50
  251.9 0.8 copy.42
  252.8 0.0 reduce-scatter.2.cloned.1.call-start
  252.9 3.6 %fusion.44 = f32[256,4096]{1,0:T(8,128)S(1)} fusion(bf16[256,512]{0,1:T(8,128)(2,1)S(1)} %bitcast.100, bf16[2,4096,512]{2,1,0:T(8,128)(2,1)} %param.21), kind=kOutput, calls=%fused_computation.45 | convolution fusion | flops 1073741824 | bytes 8650752 | tf_op jit(solution)/shard_map/dot_general | solution.py:182
  256.6 5.0 %fusion.42 = bf16[256,4096]{1,0:T(8,128)(2,1)} fusion(bf16[256,4096]{1,0:T(8,128)(2,1)S(1)} %copy-done, f32[256,4096]{1,0:T(8,128)S(1)} %fusion.44, bf16[256,512]{0,1:T(8,128)(2,1)S(1)} %bitcast.99, bf16[2,4096,512]{2,1,0:T(8,128)(2,1)} %param.21, pred[]{:T(512)S(6)} %lt.14), kind=kOutput, calls=%fused_computation.43 | convolution fusion | flops 1075838976 | bytes 12845057 | tf_op jit(solution)/shard_map/dot_general | solution.py:184
  261.6 23.6 %all-reduce.8.cloned.1.call-done = bf16[256,512]{1,0:T(8,128)(2,1)} async-done(((bf16[256,512]{1,0:T(8,128)(2,1)}), bf16[256,512]{1,0:T(8,128)(2,1)}) %all-reduce.8.cloned.1.call-update) | async-done | bytes 262160 | tf_op jit(solution)/shard_map/psum | solution.py:177
  285.2 45.5 %reduce-scatter.2.cloned.1.call-done = bf16[256,512]{1,0:T(8,128)(2,1)} async-done(((bf16[256,4096]{1,0:T(8,128)(2,1)}), bf16[256,512]{1,0:T(8,128)(2,1)}) %reduce-scatter.2.cloned.1.call-update) | async-done | bytes 262160 | tf_op jit(solution)/shard_map/reduce_scatter | solution.py:186
  330.8 2.0 broadcast_select_fusion
  (42 shorter events, 0.2 us)
Async XLA Ops:
  8.0 10.7 %copy-start.9 = (bf16[256,512]{1,0:T(8,128)(2,1)S(1)}, bf16[256,512]{1,0:T(8,128)(2,1)}, u32[]{:S(2)}) copy-start(bf16[256,512]{1,0:T(8,128)(2,1)} %param.16) | copy-start | bytes 786436
  8.0 10.7 %copy-start.13 = (s32[2,1024]{1,0:T(2,128)S(1)}, s32[2,1024]{1,0:T(2,128)}, u32[]{:S(2)}) copy-start(s32[2,1024]{1,0:T(2,128)} %param.22) | copy-start | bytes 24580
  8.0 10.7 %copy-start.14 = (s32[8]{0:T(128)S(1)}, s32[8]{0:T(128)}, u32[]{:S(2)}) copy-start(s32[8]{0:T(128)} %param.23) | copy-start | bytes 100
  8.0 22.3 %all-gather.7.cloned.1.call-start = ((), (), s32[]{:S(2)}) async-start(), calls=%async_computation.3 | async-start | bytes 1310720 | tf_op jit(solution)/shard_map/all_gather | solution.py:108
  8.8 158.6 %all-reduce.4.cloned.1.call-start = ((), (), s32[]{:S(2)}) async-start(), calls=%async_computation.2 | async-start | bytes 4194304 | tf_op jit(solution)/shard_map/psum | solution.py:84
  10.2 3.7 %collective-permute-start = (bf16[2,127,512]{1,2,0:T(8,128)(2,1)S(1)}, bf16[2,127,512]{1,2,0:T(8,128)(2,1)S(1)}, u32[]{:S(2)}, u32[]{:S(2)}) collective-permute-start(bf16[2,127,512]{1,2,0:T(8,128)(2,1)S(1)} %get-tuple-element.186), channel_id=1, source_target_pairs={{0,8},{8,16},{16,24},{1,9},{9,17},{17,25},{2,10},{10,18},{18,26},{... | collective-permute-start | bytes 780296 | tf_op jit(solution)/shard_map/ppermute | solution.py:18
  12.6 5.5 %collective-permute-start.1 = (bf16[2,127,512]{1,2,0:T(8,128)(2,1)S(1)}, bf16[2,127,512]{1,2,0:T(8,128)(2,1)S(1)}, u32[]{:S(2)}, u32[]{:S(2)}) collective-permute-start(bf16[2,127,512]{1,2,0:T(8,128)(2,1)S(1)} %get-tuple-element.187), channel_id=1, source_target_pairs={{8,0},{16,8},{24,16},{9,1},{17,9},{25,17},{10,2},{18,10},{26,18},{... | collective-permute-start | bytes 780296 | tf_op jit(solution)/shard_map/ppermute | solution.py:20
  27.2 1.3 copy-start.2
  28.6 138.8 %all-gather.5.cloned.1.call-start = ((), (), s32[]{:S(2)}) async-start(), calls=%async_computation.1 | async-start | bytes 2359296 | tf_op jit(solution)/shard_map/all_gather | solution.py:53
  29.4 165.5 %all-gather.9.cloned.1.call-start = ((), (), s32[]{:S(2)}) async-start(), calls=%async_computation.4 | async-start | bytes 2359296 | tf_op jit(solution)/shard_map/all_gather | solution.py:54
  30.1 195.7 %all-reduce.6.cloned.1.call-start = ((), (), s32[]{:S(2)}) async-start(), calls=%async_computation.6 | async-start | bytes 524288 | tf_op jit(solution)/shard_map/psum | solution.py:128
  31.4 148.7 %copy-start.3 = (bf16[256,512]{0,1:T(8,128)(2,1)}, bf16[256,512]{0,1:T(8,128)(2,1)S(1)}, u32[]{:S(2)}) copy-start(bf16[256,512]{0,1:T(8,128)(2,1)S(1)} %copy.34) | copy-start | bytes 786436
  171.8 5.2 %copy-start.1 = (bf16[2,4096,512]{2,1,0:T(8,128)(2,1)S(1)}, bf16[2,4096,512]{2,1,0:T(8,128)(2,1)}, u32[]{:S(2)}) copy-start(bf16[2,4096,512]{2,1,0:T(8,128)(2,1)} %get-tuple-element.147) | copy-start | bytes 25165828 | tf_op jit(solution)/shard_map/cond
  180.1 6.6 %copy-start.5 = (bf16[256,8,64]{0,2,1:T(8,128)(2,1)}, bf16[256,8,64]{0,2,1:T(8,128)(2,1)S(1)}, u32[]{:S(2)}) copy-start(bf16[256,8,64]{0,2,1:T(8,128)(2,1)S(1)} %get-tuple-element.156) | copy-start | bytes 786436
  180.1 14.6 %copy-start.11 = (bf16[256,8,64]{0,2,1:T(8,128)(2,1)}, bf16[256,8,64]{0,2,1:T(8,128)(2,1)S(1)}, u32[]{:S(2)}) copy-start(bf16[256,8,64]{0,2,1:T(8,128)(2,1)S(1)} %get-tuple-element.157) | copy-start | bytes 786436
  194.8 49.7 %all-gather.11.cloned.1.call-start = ((), (), s32[]{:S(2)}) async-start(), calls=%async_computation.5 | async-start | bytes 1310720 | tf_op jit(solution)/shard_map/all_gather | solution.py:139
  195.1 0.7 copy-start.12
  195.8 89.4 %all-reduce.8.cloned.1.call-start = ((), (), s32[]{:S(2)}) async-start(), calls=%async_computation.8 | async-start | bytes 524288 | tf_op jit(solution)/shard_map/psum | solution.py:177
  249.5 1.7 copy-start.6
  249.5 2.0 copy-start.4
  252.8 78.0 %reduce-scatter.2.cloned.1.call-start = ((), (), s32[]{:S(2)}) async-start(), calls=%async_computation.7 | async-start | bytes 2359296 | tf_op jit(solution)/shard_map/reduce_scatter | solution.py:186
  252.8 3.7 %copy-start = (bf16[256,4096]{1,0:T(8,128)(2,1)S(1)}, bf16[256,4096]{1,0:T(8,128)(2,1)}, u32[]{:S(2)}) copy-start(bf16[256,4096]{1,0:T(8,128)(2,1)} %get-tuple-element.198) | copy-start | bytes 6291460
  252.8 3.7 %copy-start.10 = (bf16[8,64,256]{2,1,0:T(8,128)(2,1)S(1)}, bf16[8,64,256]{2,1,0:T(8,128)(2,1)}, u32[]{:S(2)}) copy-start(bf16[8,64,256]{2,1,0:T(8,128)(2,1)} %convolution_convert_fusion) | copy-start | bytes 786436
  256.5 74.2 %copy-start.7 = (bf16[256,512]{1,0:T(8,128)(2,1)S(1)}, bf16[256,512]{1,0:T(8,128)(2,1)}, u32[]{:S(2)}) copy-start(bf16[256,512]{1,0:T(8,128)(2,1)} %param.18) | copy-start | bytes 786436
  256.5 74.2 %copy-start.8 = (bf16[256,512]{1,0:T(8,128)(2,1)S(1)}, bf16[256,512]{1,0:T(8,128)(2,1)}, u32[]{:S(2)}) copy-start(bf16[256,512]{1,0:T(8,128)(2,1)} %param.19) | copy-start | bytes 786436
Sparse Core Ops, SparseCore 0:
  10.4 19.7 all-gather.6
  32.2 71.5 all-gather.4
  105.9 66.6 all-gather.8
  194.9 30.8 all-reduce.5
  227.8 16.6 all-gather.10
  252.9 32.2 all-reduce.7
Sparse Core Ops, SparseCore 1:
  28.7 138.7 all-reduce.3
  261.7 69.0 reduce-scatter.1
where the time goes:
time: 341 us; the launch traced here: 340 us
  waiting for transfers between devices  259 us (76%)
  matrix products  28.6 us (8%)
  between operations  15.9 us (5%)
  blocking collectives  12.4 us (4%)
  local copies, waits for them, and re-layouts  11.3 us (3%)
  other arithmetic  8.97 us (3%)
  starting transfers between devices  4.03 us (1%)
    psum x1, waiting for transfers between devices, shards(): lax.psum(head_partial.astype(jnp.bfloat16), 'mp').astype(jnp.float32)  136 us
    reduce_scatter x1, waiting for transfers between devices, shards(): lax.psum_scatter(final_term.astype(jnp.bfloat16), 'mp', scatter_dimension...  45.5 us
    psum x1, waiting for transfers between devices, shards(): context_all = lax.psum(partial_ctx.astype(jnp.bfloat16), 'seq')  29.9 us
    psum x1, waiting for transfers between devices, shards(): lax.psum(query_terms.reshape(dec_tokens, col_count).astype(jnp.bfloat16),...  23.6 us
    all_gather x1, waiting for transfers between devices, shards(): grad_all = lax.all_gather(grad_own, 'seq', axis=0, tiled=True)[enc_tokens:]  17.2 us
  transfers between devices with their start and end apart: 10, of which 6 were waited for; matrix products, arithmetic and copies ran while one was open for 10% of the time, Pallas kernels for 0%

commit v1 on v0

--- a/solution.py
+++ b/solution.py
@@ -5,6 +5,27 @@
 
 HD = 64
 WIN = 127
+
+
+def ring_gather(x, axis, dim):
+    length, index, rows = (lax.axis_size(axis), lax.axis_index(axis), x.shape[dim])
+    upward = [(i, (i + 1) % length) for i in range(length)]
+    backward = [(i, (i - 1) % length) for i in range(length)]
+    out = jnp.zeros((*x.shape[:dim], length * rows, *x.shape[dim + 1 :]), x.dtype)
+    out = lax.dynamic_update_slice_in_dim(out, x, index * rows, axis=dim)
+    from_left = from_right = x
+    half = length // 2
+    for step in range(1, half + 1):
+        from_left = lax.ppermute(from_left, axis, upward)
+        out = lax.dynamic_update_slice_in_dim(
+            out, from_left, (index - step) % length * rows, axis=dim
+        )
+        if step < length - half:
+            from_right = lax.ppermute(from_right, axis, backward)
+            out = lax.dynamic_update_slice_in_dim(
+                out, from_right, (index + step) % length * rows, axis=dim
+            )
+    return out
 
 
 def with_halo(cells, sides, width):
@@ -136,7 +157,7 @@
     grad_own = lax.cond(
         is_enc, lambda: jnp.zeros((row_count, col_count), jnp.bfloat16), context_gradient
     )
-    grad_all = lax.all_gather(grad_own, "seq", axis=0, tiled=True)[enc_tokens:]
+    grad_all = ring_gather(grad_own, "seq", 0)[enc_tokens:]
     grad_heads = grad_all.reshape(dec_tokens, head_count, HD)
     row_dots = jnp.einsum(
         "qhd,qhd->hq",

time: 341 us -> 431 us (1.26)
  waiting for transfers between devices: 259 us -> 333 us
  local copies, waits for them, and re-layouts: 11.3 us -> 23.7 us
    all_gather x1, waiting for transfers between devices: 0.02 us -> 51.6 us  [shards(): lax.all_gather(cotangent, 'mp', axis=1, tiled=True)]
    all_gather x1, waiting for transfers between devices: 0.01 us -> 51.6 us  [shards(): lax.all_gather(residual, 'mp', axis=1, tiled=True)]
    psum x1, waiting for transfers between devices: 136 us -> 99.1 us  [shards(): lax.psum(head_partial.astype(jnp.bfloat16), 'mp').astype(jnp.float32)]
    reduce_scatter x1, waiting for transfers between devices: 45.5 us -> 72.4 us  [shards(): lax.psum_scatter(final_term.astype(jnp.bfloat16), 'mp', scatter_dimension...]
    all_gather x1 -> x0, waiting for transfers between devices: 17.2 us -> none  [shards(): grad_all = lax.all_gather(grad_own, 'seq', axis=0, tiled=True)[enc_tokens:]]
    dynamic_update_slice x0 -> x4, local copies, waits for them, and re-layouts: none -> 6.8 us  [the longest x2 3.41 us: ring_gather(): lax.dynamic_update_slice_in_dim(out, from_left, (index - step) % length *...]
    ppermute x0 -> x3, local copies, waits for them, and re-layouts: none -> 5.41 us  [the longest x2 3.61 us: ring_gather(): from_left = lax.ppermute(from_left, axis, upward)]
    psum x1, waiting for transfers between devices: 29.9 us -> 25.4 us  [shards(): context_all = lax.psum(partial_ctx.astype(jnp.bfloat16), 'seq')]
  transfers between devices with their start and end apart: 10 -> 12, of which waited for: 6 -> 8; matrix products, arithmetic and copies ran while one was open for 10% -> 11% of each run, Pallas kernels for 0% -> 0%
where the time goes in v1:
time: 431 us
  waiting for transfers between devices  333 us (77%)
  matrix products  29.5 us (7%)
  local copies, waits for them, and re-layouts  23.7 us (5%)
  between operations  14.5 us (3%)
  blocking collectives  12.5 us (3%)
  other arithmetic  9.06 us (2%)
  starting transfers between devices  8.27 us (2%)
    psum x1, waiting for transfers between devices, shards(): lax.psum(head_partial.astype(jnp.bfloat16), 'mp').astype(jnp.float32)  99.1 us
    reduce_scatter x1, waiting for transfers between devices, shards(): lax.psum_scatter(final_term.astype(jnp.bfloat16), 'mp', scatter_dimension...  72.4 us
    all_gather x1, waiting for transfers between devices, shards(): lax.all_gather(cotangent, 'mp', axis=1, tiled=True)  51.6 us
    all_gather x1, waiting for transfers between devices, shards(): lax.all_gather(residual, 'mp', axis=1, tiled=True)  51.6 us
    psum x1, waiting for transfers between devices, shards(): lax.psum(query_terms.reshape(dec_tokens, col_count).astype(jnp.bfloat16),...  25.7 us
    psum x1, waiting for transfers between devices, shards(): context_all = lax.psum(partial_ctx.astype(jnp.bfloat16), 'seq')  25.4 us
  transfers between devices with their start and end apart: 12, of which 8 were waited for; matrix products, arithmetic and copies ran while one was open for 11% of the time, Pallas kernels for 0%

profile of v1, /device:TPU:0, one launch (start us, length us, event | category | flops | bytes accessed | tf_op | source)
XLA Modules:
  0.0 430.7 jit_solution(17019012001093195140)
XLA Ops:
  7.2 0.7 all-gather.6.cloned.1.call-update
  8.0 0.7 all-gather.8.cloned.1.call-update
  8.7 1.2 copy.33
  10.0 0.1 fusion.57
  10.1 2.4 collective-permute-start
  12.5 1.3 collective-permute-start.1
  13.9 4.2 collective-permute-done.1
  18.0 0.5 pad_maximum_fusion
  18.6 8.5 %conditional.4 = (bf16[256,4096]{1,0:T(8,128)(2,1)S(1)}) conditional(s32[]{:T(128)} %convert_element_type.114, () %tuple.44, (s32[]{:T(128)}, s32[2,1024]{1,0:T(2,128)S(1)}, s32[]{:T(128)}, s32[]{:T(128)}, s32[256]{0:T(256)S(1)}, /*index=5*/s32[8]{0:T(128)S(1)}, bf16[256,512]{1,0:T(8,128)(2,1)S(1)}, bf16[2,510,512]{1,2,0:T(8,128)(2,1)S(1)}, ...), branch_computations={%region_0.0_spmd, %region_1.4_spmd} | conditional | flops 1489188096 | bytes 13526612 | solution.py:102
  18.7 0.1 constant_dynamic-slice_fusion
  18.8 0.2 compare_and_fusion
  19.0 0.1 copy.36
  19.1 0.1 subtract_abs_fusion
  19.3 2.0 fusion.56
  21.4 2.3 fusion.11
  23.7 3.5 fusion.1
  27.1 1.4 copy-done.2
  28.6 0.5 all-gather.4.cloned.1.call-update
  29.2 0.1 compare_and_fusion.1
  29.3 0.8 all-gather.6.cloned.1.call-done
  30.1 1.0 slice.85
  31.1 0.1 copy.37
  31.2 51.6 %all-gather.8.cloned.1.call-done = bf16[256,4096]{1,0:T(8,128)(2,1)} async-done(((bf16[256,512]{1,0:T(8,128)(2,1)}), bf16[256,4096]{1,0:T(8,128)(2,1)}) %all-gather.8.cloned.1.call-update) | async-done | bytes 2097168 | tf_op jit(solution)/shard_map/all_gather | solution.py:75
  82.8 0.7 conditional.6
  82.8 0.7 broadcast.153
  83.6 4.3 collective-permute-start.3
  87.9 99.1 %all-reduce.4.cloned.1.call-done = bf16[256,4096]{1,0:T(8,128)(2,1)} async-done(((bf16[256,4096]{1,0:T(8,128)(2,1)}), bf16[256,4096]{1,0:T(8,128)(2,1)}) %all-reduce.4.cloned.1.call-update) | async-done | bytes 2097168 | tf_op jit(solution)/shard_map/psum | solution.py:105
  187.0 51.6 %all-gather.4.cloned.1.call-done = bf16[256,4096]{1,0:T(8,128)(2,1)} async-done(((bf16[256,512]{1,0:T(8,128)(2,1)}), bf16[256,4096]{1,0:T(8,128)(2,1)}) %all-gather.4.cloned.1.call-update) | async-done | bytes 2097168 | tf_op jit(solution)/shard_map/all_gather | solution.py:74
  238.5 4.3 %add_convert_fusion = bf16[256,4096]{1,0:T(8,128)(2,1)} fusion(bf16[256,4096]{1,0:T(8,128)(2,1)} %all-reduce.4.cloned.1.call-done, bf16[256,4096]{1,0:T(8,128)(2,1)} %all-gather.4.cloned.1.call-done), kind=kLoop, calls=%fused_computation.49 | loop fusion | flops 4194304 | bytes 6291456 | tf_op jit(solution)/shard_map/convert_element_type | solution.py:106
  242.9 8.5 %conditional.5 = (bf16[256,8,64]{0,2,1:T(8,128)(2,1)S(1)}, bf16[256,8,64]{0,2,1:T(8,128)(2,1)S(1)}) conditional(s32[]{:T(128)} %convert_element_type.114, () %tuple.46, (bf16[2,4096,512]{2,1,0:T(8,128)(2,1)}, bf16[256,4096]{1,0:T(8,128)(2,1)}) %tuple.47), branch_computations={%region_5.6_spmd, %region_6.7_spmd} | conditional | flops 2147745792 | bytes 47710252 | solution.py:120
  242.9 4.2 fusion.29
  247.1 1.0 copy-done.1
  248.1 2.8 fusion.26
  250.9 0.1 copy.31
  251.1 0.1 copy.32
  251.4 0.5 fusion.59
  251.9 5.8 %pmax.7 = f32[8,256]{1,0:T(8,128)S(1)} all-reduce(f32[8,256]{1,0:T(8,128)S(1)} %get-tuple-element.164), channel_id=1, replica_groups=mesh['seq'=4,'mp'=8] {'seq'}, use_global_device_ids=true, to_apply=%region_8.9 | all-reduce | flops 2048 | bytes 16384 | tf_op jit(solution)/shard_map/pmax | solution.py:141
  257.7 0.3 fusion.49
  258.0 6.7 %psum.29 = f32[8,256]{1,0:T(8,128)S(1)} all-reduce(f32[8,256]{1,0:T(8,128)S(1)} %fusion.49), channel_id=1, replica_groups=mesh['seq'=4,'mp'=8] {'seq'}, use_global_device_ids=true, to_apply=%region_10.11 | all-reduce | flops 2048 | bytes 16384 | tf_op jit(solution)/shard_map/psum | solution.py:143
  264.7 0.3 fusion.52
  265.1 2.0 convolution_convert_fusion.1
  267.2 1.8 copy.38
  269.0 1.1 broadcast_in_dim.29
  270.1 1.7 constant_dynamic-update-slice_fusion.3
  271.8 25.4 %all-reduce.6.cloned.1.call-done = bf16[256,512]{0,1:T(8,128)(2,1)} async-done(((bf16[256,512]{0,1:T(8,128)(2,1)}), bf16[256,512]{0,1:T(8,128)(2,1)}) %all-reduce.6.cloned.1.call-update) | async-done | bytes 262160 | tf_op jit(solution)/shard_map/psum | solution.py:149
  297.2 1.6 conditional.7
  297.2 1.6 broadcast.154
  298.7 1.8 copy.39
  300.5 1.8 copy.40
  302.3 1.7 constant_dynamic-update-slice_fusion.2
  304.0 1.7 constant_dynamic-update-slice_fusion.1
  305.7 1.8 copy.41
  307.5 1.7 constant_dynamic-update-slice_fusion
  309.3 1.1 fusion.53
  310.4 1.1 convolution_convert_fusion
  311.5 1.7 multiply_convert_fusion
  313.2 0.3 fusion.51
  313.5 0.4 fusion.50
  313.9 0.8 copy.48
  314.9 3.6 fusion.44
  318.6 5.0 %fusion.42 = bf16[256,4096]{1,0:T(8,128)(2,1)} fusion(bf16[256,4096]{1,0:T(8,128)(2,1)S(1)} %copy-done, f32[256,4096]{1,0:T(8,128)S(1)} %fusion.44, bf16[256,512]{0,1:T(8,128)(2,1)S(1)} %bitcast.95, bf16[2,4096,512]{2,1,0:T(8,128)(2,1)} %param.21, pred[]{:T(512)S(6)} %lt.36), kind=kOutput, calls=%fused_computation.43 | convolution fusion | flops 1075838976 | bytes 12845057 | tf_op jit(solution)/shard_map/dot_general | solution.py:205
  323.7 25.7 %all-reduce.8.cloned.1.call-done = bf16[256,512]{1,0:T(8,128)(2,1)} async-done(((bf16[256,512]{1,0:T(8,128)(2,1)}), bf16[256,512]{1,0:T(8,128)(2,1)}) %all-reduce.8.cloned.1.call-update) | async-done | bytes 262160 | tf_op jit(solution)/shard_map/psum | solution.py:198
  349.4 72.4 %reduce-scatter.2.cloned.1.call-done = bf16[256,512]{1,0:T(8,128)(2,1)} async-done(((bf16[256,4096]{1,0:T(8,128)(2,1)}), bf16[256,512]{1,0:T(8,128)(2,1)}) %reduce-scatter.2.cloned.1.call-update) | async-done | bytes 262160 | tf_op jit(solution)/shard_map/reduce_scatter | solution.py:207
  421.8 2.0 broadcast_select_fusion
  (46 shorter events, 0.5 us)
Async XLA Ops:
  7.2 11.4 %copy-start.7 = (bf16[256,512]{1,0:T(8,128)(2,1)S(1)}, bf16[256,512]{1,0:T(8,128)(2,1)}, u32[]{:S(2)}) copy-start(bf16[256,512]{1,0:T(8,128)(2,1)} %param.16) | copy-start | bytes 786436
  7.2 11.4 %copy-start.10 = (s32[2,1024]{1,0:T(2,128)S(1)}, s32[2,1024]{1,0:T(2,128)}, u32[]{:S(2)}) copy-start(s32[2,1024]{1,0:T(2,128)} %param.22) | copy-start | bytes 24580
  7.2 11.4 %copy-start.11 = (s32[8]{0:T(128)S(1)}, s32[8]{0:T(128)}, u32[]{:S(2)}) copy-start(s32[8]{0:T(128)} %param.23) | copy-start | bytes 100
  7.2 22.9 %all-gather.6.cloned.1.call-start = ((), (), s32[]{:S(2)}) async-start(), calls=%async_computation.3 | async-start | bytes 1310720 | tf_op jit(solution)/shard_map/all_gather | solution.py:129
  7.9 74.9 %all-gather.8.cloned.1.call-start = ((), (), s32[]{:S(2)}) async-start(), calls=%async_computation.4 | async-start | bytes 2359296 | tf_op jit(solution)/shard_map/all_gather | solution.py:75
  8.7 178.3 %all-reduce.4.cloned.1.call-start = ((), (), s32[]{:S(2)}) async-start(), calls=%async_computation.2 | async-start | bytes 4194304 | tf_op jit(solution)/shard_map/psum | solution.py:105
  10.1 3.7 collective-permute-start
  12.5 5.5 %collective-permute-start.1 = (bf16[2,127,512]{1,2,0:T(8,128)(2,1)S(1)}, bf16[2,127,512]{1,2,0:T(8,128)(2,1)S(1)}, u32[]{:S(2)}, u32[]{:S(2)}) collective-permute-start(bf16[2,127,512]{1,2,0:T(8,128)(2,1)S(1)} %get-tuple-element.161), channel_id=1, source_target_pairs={{8,0},{16,8},{24,16},{9,1},{17,9},{25,17},{10,2},{18,10},{26,18},{... | collective-permute-start | bytes 780296 | tf_op jit(solution)/shard_map/ppermute | solution.py:41
  27.1 1.4 copy-start.2
  28.5 210.0 %all-gather.4.cloned.1.call-start = ((), (), s32[]{:S(2)}) async-start(), calls=%async_computation.1 | async-start | bytes 2359296 | tf_op jit(solution)/shard_map/all_gather | solution.py:74
  29.1 268.1 %all-reduce.6.cloned.1.call-start = ((), (), s32[]{:S(2)}) async-start(), calls=%async_computation.5 | async-start | bytes 524288 | tf_op jit(solution)/shard_map/psum | solution.py:149
  83.6 217.0 %collective-permute-start.3 = (bf16[256,512]{1,0:T(8,128)(2,1)}, bf16[256,512]{1,0:T(8,128)(2,1)}, u32[]{:S(2)}, u32[]{:S(2)}) collective-permute-start(bf16[256,512]{1,0:T(8,128)(2,1)} %get-tuple-element.171), channel_id=1, source_target_pairs={{0,24},{8,0},{16,8},{24,16},{1,25},{9,1},{17,9},{25,17},{2,26},{10... | collective-permute-start | bytes 786440 | tf_op jit(solution)/shard_map/ppermute | solution.py:24
  87.9 181.1 %collective-permute-start.2 = (bf16[256,512]{1,0:T(8,128)(2,1)}, bf16[256,512]{1,0:T(8,128)(2,1)}, u32[]{:S(2)}, u32[]{:S(2)}) collective-permute-start(bf16[256,512]{1,0:T(8,128)(2,1)} %get-tuple-element.171), channel_id=1, source_target_pairs={{0,8},{8,16},{16,24},{24,0},{1,9},{9,17},{17,25},{25,1},{2,10},{10... | collective-permute-start | bytes 786440 | tf_op jit(solution)/shard_map/ppermute | solution.py:19
  242.9 5.2 %copy-start.1 = (bf16[2,4096,512]{2,1,0:T(8,128)(2,1)S(1)}, bf16[2,4096,512]{2,1,0:T(8,128)(2,1)}, u32[]{:S(2)}) copy-start(bf16[2,4096,512]{2,1,0:T(8,128)(2,1)} %get-tuple-element.117) | copy-start | bytes 25165828 | tf_op jit(solution)/shard_map/cond
  251.4 6.6 %copy-start.3 = (bf16[256,8,64]{0,2,1:T(8,128)(2,1)}, bf16[256,8,64]{0,2,1:T(8,128)(2,1)S(1)}, u32[]{:S(2)}) copy-start(bf16[256,8,64]{0,2,1:T(8,128)(2,1)S(1)} %get-tuple-element.126) | copy-start | bytes 786436
  251.4 6.6 %copy-start.9 = (bf16[256,8,64]{0,2,1:T(8,128)(2,1)}, bf16[256,8,64]{0,2,1:T(8,128)(2,1)S(1)}, u32[]{:S(2)}) copy-start(bf16[256,8,64]{0,2,1:T(8,128)(2,1)S(1)} %get-tuple-element.127) | copy-start | bytes 786436
  267.0 82.4 %all-reduce.8.cloned.1.call-start = ((), (), s32[]{:S(2)}) async-start(), calls=%async_computation.7 | async-start | bytes 524288 | tf_op jit(solution)/shard_map/psum | solution.py:198
  269.0 36.8 %collective-permute-start.4 = (bf16[256,512]{1,0:T(8,128)(2,1)}, bf16[256,512]{1,0:T(8,128)(2,1)}, u32[]{:S(2)}, u32[]{:S(2)}) collective-permute-start(bf16[256,512]{1,0:T(8,128)(2,1)} %collective-permute-done.2), channel_id=1, source_target_pairs={{0,8},{8,16},{16,24},{24,0},{1,9},{9,17},{17,25},{25,1},{2,10},{10... | collective-permute-start | bytes 786440 | tf_op jit(solution)/shard_map/ppermute | solution.py:19
  311.5 1.7 copy-start.4
  314.8 107.0 %reduce-scatter.2.cloned.1.call-start = ((), (), s32[]{:S(2)}) async-start(), calls=%async_computation.6 | async-start | bytes 2359296 | tf_op jit(solution)/shard_map/reduce_scatter | solution.py:207
  314.9 3.7 copy-start
  314.9 3.7 copy-start.8
  318.6 103.3 %copy-start.5 = (bf16[256,512]{1,0:T(8,128)(2,1)S(1)}, bf16[256,512]{1,0:T(8,128)(2,1)}, u32[]{:S(2)}) copy-start(bf16[256,512]{1,0:T(8,128)(2,1)} %param.19) | copy-start | bytes 786436
  318.6 103.3 %copy-start.6 = (bf16[256,512]{1,0:T(8,128)(2,1)S(1)}, bf16[256,512]{1,0:T(8,128)(2,1)}, u32[]{:S(2)}) copy-start(bf16[256,512]{1,0:T(8,128)(2,1)} %param.18) | copy-start | bytes 786436
Sparse Core Ops, SparseCore 0:
  9.6 20.4 all-gather.5
  32.1 50.6 all-gather.7
  86.5 100.4 all-reduce.3
  188.9 49.6 all-gather.3
  267.2 29.9 all-reduce.5
  314.9 34.4 all-reduce.7
  352.9 68.8 reduce-scatter.1
